TPU v7x, 256 devices: a whole 4x4x8 slice. The times are simulated.
256 devices in a mesh: row: 32 (over y, z), col: 8 (over x, core).
Axes of the slice: x: 4, y: 4, z: 8, core: 2. Of those that a mesh axis runs over, the one named last changes fastest.
Arguments:
- query_acts: bfloat16 [256, 8192], P('col', 'row'), may hold values from -6 to 6
- query_grads: bfloat16 [256, 28672], P('row', 'col'), may hold values from -6 to 6
- ritz_mats: float32 [3, 8192, 28672], P(None, 'row', 'col'), may hold values from -0.095683193 to 0.095683193, as said below
- eigenvalues: float32 [3], replicated, may hold values from 0.5 to 4
- train_acts: bfloat16 [256, 8192], P('row'), may hold values from -6 to 6
- train_grads: bfloat16 [256, 28672], P('row', 'col'), may hold values from -6 to 6
Outputs:
- response: bfloat16 [256, 28672], P('row', 'col')
- scores: float32 [256], P('row')
Inputs may be any that keep to these rules, and one draw needn't show every extreme that they name: `ritz_mats`: real entries of order one over the square root of 8192; every matrix has full rank.
All inputs are finite; a program needn't handle non-finite values.
Results may differ from a plain program's by a relative error of at most 0.0012.
Values may be sent and summed in bfloat16 or wider, within the bound.
A program may use at most 64 MiB of HBM per device.

v0:
```python
import math
import jax
import jax.numpy as jnp
from jax import lax
from jax.sharding import PartitionSpec as P

D_OUT = 28672
QUERY = 256
highest = lax.Precision.HIGHEST


def per_device(query_acts, query_grads, ritz_mats, eigenvalues, train_acts, train_grads):
    acts_all = lax.all_gather(query_acts, "col", axis=0, tiled=True)
    grad_tile = lax.dot_general(
        acts_all,
        lax.all_gather(query_grads, "row", axis=0, tiled=True),
        (((0,), (0,)), ((), ())),
        preferred_element_type=jnp.float32,
    )
    local_terms = jnp.sum(ritz_mats * grad_tile[None], axis=(1, 2))
    coeffs = lax.psum(local_terms, ("row", "col"))
    weights = coeffs / (eigenvalues * math.sqrt(QUERY * D_OUT))
    train_local = lax.all_to_all(train_acts, "row", split_axis=1, concat_axis=0, tiled=True).astype(
        jnp.float32
    )
    combined = jnp.tensordot(weights, ritz_mats, axes=1, precision=highest)
    root_width = math.sqrt(D_OUT)
    response_full = lax.psum_scatter(
        jnp.dot(train_local, combined, precision=highest), "row", scatter_dimension=0, tiled=True
    )
    score_terms = jnp.sum(response_full * train_grads.astype(jnp.float32), axis=1) / root_width
    scores = lax.psum(score_terms, "col")
    response = response_full.astype(jnp.bfloat16)
    return (response, scores)


def solution(mesh):
    in_specs = (
        P("col", "row"),
        P("row", "col"),
        P(None, "row", "col"),
        P(),
        P("row", None),
        P("row", "col"),
    )
    out_specs = (P("row", "col"), P("row"))
    return jax.shard_map(
        per_device, mesh=mesh, in_specs=in_specs, out_specs=out_specs, check_vma=False
    )
```

profile of v0, /device:TPU:1, one launch (start us, length us, event | category | flops | bytes accessed | tf_op | source)
XLA Modules:
  0.0 477.4 jit_solution(8239477549064250648)
XLA Ops:
  7.2 0.0 all-gather.2.cloned.1.call-start
  7.2 0.7 all-gather.2.cloned.1.call-update
  7.9 16.0 %all_gather.6 = bf16[256,256]{1,0:T(8,128)(2,1)S(1)} all-gather(bf16[32,256]{1,0:T(8,128)(2,1)} %param.6), channel_id=1, replica_groups=mesh['row'=32,'col'=8] {'col'}, dimensions={0}, use_global_device_ids=true | all-gather | bytes 147456 | tf_op jit(solution)/shard_map/all_gather | solution.py:13
  23.9 64.0 %all-gather.2.cloned.1.call-done = bf16[256,3584]{1,0:T(8,128)(2,1)} async-done(((bf16[8,3584]{1,0:T(8,128)(2,1)}), bf16[256,3584]{1,0:T(8,128)(2,1)}) %all-gather.2.cloned.1.call-update) | async-done | bytes 1835024 | tf_op jit(solution)/shard_map/all_gather | solution.py:16
  87.9 2.2 fusion.8
  90.1 0.0 copy-start.1
  90.1 5.3 %multiply_reduce_fusion = f32[3]{0:T(128)S(1)} fusion(f32[3,256,3584]{2,1,0:T(8,128)} %param.8, f32[256,3584]{1,0:T(8,128)S(1)} %fusion.8), kind=kLoop, calls=%fused_computation.2 | loop fusion | flops 5505021 | bytes 14680076 | tf_op jit(solution)/shard_map/reduce_sum | solution.py:20
  95.4 5.3 %all-to-all-start = ((bf16[8,32,256]{2,0,1:T(8,128)(2,1)}), bf16[8,32,256]{2,0,1:T(8,128)(2,1)S(1)}, u32[]{:S(2)}, u32[]{:S(2)}) async-start(bf16[8,32,256]{2,0,1:T(8,128)(2,1)} %bitcast.2), calls=%async_computation | async-start | bytes 262144 | tf_op jit(solution)/shard_map/all_to_all | solution.py:23
  100.7 0.0 reduce-scatter.4.cloned.1.call-start
  100.8 80.7 %psum.14 = f32[3]{0:T(128)S(1)} all-reduce(f32[3]{0:T(128)S(1)} %multiply_reduce_fusion), channel_id=1, replica_groups=mesh['row'=32,'col'=8] {'row','col'}, use_global_device_ids=true, to_apply=%region_1.0 | all-reduce | flops 3 | bytes 24 | tf_op jit(solution)/shard_map/psum | solution.py:21
  181.5 0.0 copy-done.1
  181.5 40.2 %fusion = f32[1,256,3584]{2,0,1:T(1,128)} fusion(f32[3,256,3584]{2,1,0:T(8,128)} %param.8, f32[3]{0:T(128)S(1)} %psum.14, f32[3]{0:T(128)S(1)} %copy-done.1), kind=kOutput, calls=%fused_computation | convolution fusion | flops 33030150 | bytes 14680088 | tf_op jit(solution)/shard_map/dot_general | solution.py:26
  221.7 0.0 all-to-all-done
  221.7 6.9 %convolution_bitcast_fusion = f32[256,3584]{0,1:T(8,128)} fusion(f32[1,256,3584]{2,0,1:T(1,128)} %fusion, bf16[8,32,256]{2,0,1:T(8,128)(2,1)S(1)} %all-to-all-done), kind=kOutput, calls=%fused_computation.3 | convolution fusion | flops 2818572288 | bytes 7471104 | tf_op jit(solution)/shard_map/dot_general | solution.py:29
  228.6 5.2 %copy.14 = f32[256,3584]{1,0:T(8,128)} copy(f32[256,3584]{0,1:T(8,128)} %convolution_bitcast_fusion) | data formatting | bytes 7340032
  233.7 0.0 copy-start
  233.7 0.0 reduce-scatter.4.cloned.1.call-update
  233.8 0.8 copy-done
  234.6 0.3 copy.10
  234.9 211.5 %reduce-scatter.4.cloned.1.call-done = f32[8,3584]{1,0:T(8,128)} async-done(((f32[256,3584]{1,0:T(8,128)}), f32[8,3584]{1,0:T(8,128)}) %reduce-scatter.4.cloned.1.call-update) | async-done | bytes 114704
  446.4 2.7 copy.15
  449.1 2.5 multiply_reduce_fusion.1
  451.6 0.9 copy.11
  452.5 18.1 %psum.15 = f32[8]{0:T(128)} all-reduce(f32[8]{0:T(128)S(1)} %broadcast_multiply_fusion), channel_id=1, replica_groups=mesh['row'=32,'col'=8] {'col'}, use_global_device_ids=true, to_apply=%region_4.0 | all-reduce | flops 8 | bytes 64 | tf_op jit(solution)/shard_map/psum | solution.py:32
  (1 shorter events, 0.0 us)
Async XLA Ops:
  7.2 80.8 %all-gather.2.cloned.1.call-start = ((), (), s32[]{:S(2)}) async-start(), calls=%async_computation.2 | async-start | bytes 1892352 | tf_op jit(solution)/shard_map/all_gather | solution.py:16
  90.1 91.4 %copy-start.1 = (f32[3]{0:T(128)S(1)}, f32[3]{0:T(128)}, u32[]{:S(2)}) copy-start(f32[3]{0:T(128)} %param.9) | copy-start | bytes 40
  95.4 126.3 %all-to-all-start = ((bf16[8,32,256]{2,0,1:T(8,128)(2,1)}), bf16[8,32,256]{2,0,1:T(8,128)(2,1)S(1)}, u32[]{:S(2)}, u32[]{:S(2)}) async-start(bf16[8,32,256]{2,0,1:T(8,128)(2,1)} %bitcast.2), calls=%async_computation | async-start | bytes 262144 | tf_op jit(solution)/shard_map/all_to_all | solution.py:23
  100.7 345.7 %reduce-scatter.4.cloned.1.call-start = ((), (), s32[]{:S(2)}) async-start(), calls=%async_computation.3 | async-start | bytes 3784704
  233.7 0.8 copy-start
Sparse Core Ops, SparseCore 0:
  10.6 77.3 all-gather.1
  233.9 212.4 reduce-scatter.3
where the time goes:
time: 478 us; the launch traced here: 477 us
  waiting for transfers between devices  276 us (58%)
  blocking collectives  115 us (24%)
  matrix products  49.2 us (10%)
  between operations  14.1 us (3%)
  local copies, waits for them, and re-layouts  9.87 us (2%)
  other arithmetic  7.81 us (2%)
  starting transfers between devices  5.4 us (1%)
    unnamed x3, waiting for transfers between devices  212 us
    psum x1, blocking collectives, per_device(): coeffs = lax.psum(local_terms, ('row', 'col'))  80.7 us
    all_gather x1, waiting for transfers between devices, per_device(): lax.all_gather(query_grads, 'row', axis=0, tiled=True)  64 us
    dot_general x1, matrix products, per_device(): combined = jnp.tensordot(weights, ritz_mats, axes=1, precision=highest)  40.2 us
    psum x1, blocking collectives, per_device(): scores = lax.psum(score_terms, 'col')  18.1 us
    all_gather x1, blocking collectives, per_device(): acts_all = lax.all_gather(query_acts, 'col', axis=0, tiled=True)  16 us
    unnamed x7, local copies, waits for them, and re-layouts  9.57 us
  transfers between devices with their start and end apart: 3, of which 2 were waited for; matrix products, arithmetic and copies ran while one was open for 8% of the time, Pallas kernels for 0%

commit v1 on v0

--- a/solution.py
+++ b/solution.py
@@ -13,7 +13,9 @@
     acts_all = lax.all_gather(query_acts, "col", axis=0, tiled=True)
     grad_tile = lax.dot_general(
         acts_all,
-        lax.all_gather(query_grads, "row", axis=0, tiled=True),
+        jnp.concatenate(
+            lax.all_to_all(jnp.stack([query_grads] * lax.axis_size("row")), "row", 0, 0), axis=0
+        ),
         (((0,), (0,)), ((), ())),
         preferred_element_type=jnp.float32,
     )

time: 478 us -> 451 us (0.944)
  waiting for transfers between devices: 276 us -> 240 us
  starting transfers between devices: 5.4 us -> 18.7 us
  blocking collectives: 115 us -> 110 us
    all_gather x1 -> x0, waiting for transfers between devices: 64 us -> none  [per_device(): lax.all_gather(query_grads, 'row', axis=0, tiled=True)]
    all_to_all x0 -> x1, waiting for transfers between devices: none -> 29.5 us  [per_device(): lax.all_to_all(jnp.stack([query_grads] * lax.axis_size('row')), 'row', 0, 0)]
    all_to_all x0 -> x1, starting transfers between devices: none -> 12 us  [per_device(): lax.all_to_all(jnp.stack([query_grads] * lax.axis_size('row')), 'row', 0, 0)]
    unnamed x3 -> x2, waiting for transfers between devices: 212 us -> 211 us
    unnamed x7 -> x9, local copies, waits for them, and re-layouts: 9.57 us -> 9.57 us
  transfers between devices with their start and end apart: 3 -> 3, of which waited for: 2 -> 2; matrix products, arithmetic and copies ran while one was open for 8% -> 9% of each run, Pallas kernels for 0% -> 0%
where the time goes in v1:
time: 451 us
  waiting for transfers between devices  240 us (53%)
  blocking collectives  110 us (24%)
  matrix products  47.7 us (11%)
  starting transfers between devices  18.7 us (4%)
  between operations  14.1 us (3%)
  local copies, waits for them, and re-layouts  12.1 us (3%)
  other arithmetic  7.81 us (2%)
    unnamed x2, waiting for transfers between devices  211 us
    psum x1, blocking collectives, per_device(): coeffs = lax.psum(local_terms, ('row', 'col'))  77.7 us
    dot_general x1, matrix products, per_device(): combined = jnp.tensordot(weights, ritz_mats, axes=1, precision=highest)  40.2 us
    all_to_all x1, waiting for transfers between devices, per_device(): lax.all_to_all(jnp.stack([query_grads] * lax.axis_size('row')), 'row', 0, 0)  29.5 us
    psum x1, blocking collectives, per_device(): scores = lax.psum(score_terms, 'col')  18.1 us
    all_gather x1, blocking collectives, per_device(): acts_all = lax.all_gather(query_acts, 'col', axis=0, tiled=True)  13.9 us
    all_to_all x1, starting transfers between devices, per_device(): lax.all_to_all(jnp.stack([query_grads] * lax.axis_size('row')), 'row', 0, 0)  12 us
    unnamed x9, local copies, waits for them, and re-layouts  9.57 us
  transfers between devices with their start and end apart: 3, of which 2 were waited for; matrix products, arithmetic and copies ran while one was open for 9% of the time, Pallas kernels for 0%

profile of v1, /device:TPU:1, one launch (start us, length us, event | category | flops | bytes accessed | tf_op | source)
XLA Modules:
  0.0 450.5 jit_solution(10153347538467698464)
XLA Ops:
  7.2 0.0 copy-start.1
  7.2 2.2 stack.2
  9.4 12.0 %all-to-all-start = ((bf16[32,8,3584]{2,1,0:T(8,128)(2,1)}), bf16[32,8,3584]{2,1,0:T(8,128)(2,1)S(1)}, u32[]{:S(2)}, u32[]{:S(2)}) async-start(bf16[32,8,3584]{2,1,0:T(8,128)(2,1)} %stack.2), calls=%async_computation | async-start | bytes 3670016 | tf_op jit(solution)/shard_map/all_to_all | solution.py:17
  21.4 0.0 copy-done.1
  21.4 13.9 %all_gather.3 = bf16[256,256]{1,0:T(8,128)(2,1)S(1)} all-gather(bf16[32,256]{1,0:T(8,128)(2,1)S(1)} %copy-done.1), channel_id=1, replica_groups=mesh['row'=32,'col'=8] {'col'}, dimensions={0}, use_global_device_ids=true | all-gather | bytes 147456 | tf_op jit(solution)/shard_map/all_gather | solution.py:13
  35.3 29.5 %all-to-all-done = bf16[32,8,3584]{2,1,0:T(8,128)(2,1)S(1)} async-done(((bf16[32,8,3584]{2,1,0:T(8,128)(2,1)}), bf16[32,8,3584]{2,1,0:T(8,128)(2,1)S(1)}, u32[]{:S(2)}, u32[]{:S(2)}) %all-to-all-start) | async-done | bytes 1835040 | tf_op jit(solution)/shard_map/all_to_all | solution.py:17
  64.8 0.7 fusion.4
  65.5 0.0 copy-start.2
  65.5 5.3 %multiply_reduce_fusion = f32[3]{0:T(128)S(1)} fusion(f32[3,256,3584]{2,1,0:T(8,128)} %param.8, f32[256,3584]{1,0:T(8,128)S(1)} %fusion.4), kind=kLoop, calls=%fused_computation.2 | loop fusion | flops 5505021 | bytes 14680076 | tf_op jit(solution)/shard_map/reduce_sum | solution.py:22
  70.8 6.7 %all-to-all-start.1 = ((bf16[8,32,256]{2,0,1:T(8,128)(2,1)}), bf16[8,32,256]{2,0,1:T(8,128)(2,1)S(1)}, u32[]{:S(2)}, u32[]{:S(2)}) async-start(bf16[8,32,256]{2,0,1:T(8,128)(2,1)} %bitcast.3), calls=%async_computation.1 | async-start | bytes 262144 | tf_op jit(solution)/shard_map/all_to_all | solution.py:25
  77.4 0.0 reduce-scatter.4.cloned.1.call-start
  77.5 77.7 %psum.14 = f32[3]{0:T(128)S(1)} all-reduce(f32[3]{0:T(128)S(1)} %multiply_reduce_fusion), channel_id=1, replica_groups=mesh['row'=32,'col'=8] {'row','col'}, use_global_device_ids=true, to_apply=%region_1.0 | all-reduce | flops 3 | bytes 24 | tf_op jit(solution)/shard_map/psum | solution.py:23
  155.1 0.0 copy-done.2
  155.1 40.2 %fusion = f32[1,256,3584]{2,0,1:T(1,128)} fusion(f32[3,256,3584]{2,1,0:T(8,128)} %param.8, f32[3]{0:T(128)S(1)} %psum.14, f32[3]{0:T(128)S(1)} %copy-done.2), kind=kOutput, calls=%fused_computation | convolution fusion | flops 33030150 | bytes 14680088 | tf_op jit(solution)/shard_map/dot_general | solution.py:28
  195.3 0.0 all-to-all-done.1
  195.3 6.9 %convolution_bitcast_fusion = f32[256,3584]{0,1:T(8,128)} fusion(f32[1,256,3584]{2,0,1:T(1,128)} %fusion, bf16[8,32,256]{2,0,1:T(8,128)(2,1)S(1)} %all-to-all-done.1), kind=kOutput, calls=%fused_computation.3 | convolution fusion | flops 2818572288 | bytes 7471104 | tf_op jit(solution)/shard_map/dot_general | solution.py:31
  202.2 5.2 %copy.14 = f32[256,3584]{1,0:T(8,128)} copy(f32[256,3584]{0,1:T(8,128)} %convolution_bitcast_fusion) | data formatting | bytes 7340032
  207.4 0.0 copy-start
  207.4 0.0 reduce-scatter.4.cloned.1.call-update
  207.4 0.8 copy-done
  208.2 0.3 copy.10
  208.5 210.9 %reduce-scatter.4.cloned.1.call-done = f32[8,3584]{1,0:T(8,128)} async-done(((f32[256,3584]{1,0:T(8,128)}), f32[8,3584]{1,0:T(8,128)}) %reduce-scatter.4.cloned.1.call-update) | async-done | bytes 114704
  419.4 2.7 copy.15
  422.1 2.5 multiply_reduce_fusion.1
  424.6 0.9 copy.11
  425.5 18.1 %psum.15 = f32[8]{0:T(128)} all-reduce(f32[8]{0:T(128)S(1)} %broadcast_multiply_fusion), channel_id=1, replica_groups=mesh['row'=32,'col'=8] {'col'}, use_global_device_ids=true, to_apply=%region_4.0 | all-reduce | flops 8 | bytes 64 | tf_op jit(solution)/shard_map/psum | solution.py:34
  (1 shorter events, 0.0 us)
Async XLA Ops:
  7.2 14.2 %copy-start.1 = (bf16[32,256]{1,0:T(8,128)(2,1)S(1)}, bf16[32,256]{1,0:T(8,128)(2,1)}, u32[]{:S(2)}) copy-start(bf16[32,256]{1,0:T(8,128)(2,1)} %param.6) | copy-start | bytes 49156
  9.4 55.4 %all-to-all-start = ((bf16[32,8,3584]{2,1,0:T(8,128)(2,1)}), bf16[32,8,3584]{2,1,0:T(8,128)(2,1)S(1)}, u32[]{:S(2)}, u32[]{:S(2)}) async-start(bf16[32,8,3584]{2,1,0:T(8,128)(2,1)} %stack.2), calls=%async_computation | async-start | bytes 3670016 | tf_op jit(solution)/shard_map/all_to_all | solution.py:17
  65.5 89.7 %copy-start.2 = (f32[3]{0:T(128)S(1)}, f32[3]{0:T(128)}, u32[]{:S(2)}) copy-start(f32[3]{0:T(128)} %param.9) | copy-start | bytes 40
  70.8 124.6 %all-to-all-start.1 = ((bf16[8,32,256]{2,0,1:T(8,128)(2,1)}), bf16[8,32,256]{2,0,1:T(8,128)(2,1)S(1)}, u32[]{:S(2)}, u32[]{:S(2)}) async-start(bf16[8,32,256]{2,0,1:T(8,128)(2,1)} %bitcast.3), calls=%async_computation.1 | async-start | bytes 262144 | tf_op jit(solution)/shard_map/all_to_all | solution.py:25
  77.4 342.0 %reduce-scatter.4.cloned.1.call-start = ((), (), s32[]{:S(2)}) async-start(), calls=%async_computation.3 | async-start | bytes 3784704
  207.4 0.8 copy-start
Sparse Core Ops, SparseCore 0:
  207.5 211.8 reduce-scatter.3
